TPU v7x, 32 devices: a whole 2x2x4 slice. The times are simulated.
32 devices in a mesh: dp: 8 (over y, x, core), dap: 4 (over z).
Axes of the slice: x: 2, y: 2, z: 4, core: 2. Of those that a mesh axis runs over, the one named last changes fastest.
Arguments:
- pair_act: bfloat16 [8, 128, 128, 128], P('dp', 'dap'), may hold values from -6 to 6
- pair_cot: bfloat16 [8, 128, 128, 128], P('dp', 'dap'), may hold values from -6 to 6
- in_gain: float32 [128], replicated, may hold values from 0.25 to 1.75
- in_bias: float32 [128], replicated, may hold values from -3 to 3
- proj_weight: bfloat16 [128, 512], replicated, may hold values from -0.5 to 0.5
- gate_weight: bfloat16 [128, 128], replicated, may hold values from -0.5 to 0.5
- out_gain: float32 [128], replicated, may hold values from 0.25 to 1.75
- out_bias: float32 [128], replicated, may hold values from -3 to 3
- out_weight: bfloat16 [128, 128], replicated, may hold values from -0.5 to 0.5
Outputs:
- update: bfloat16 [8, 128, 128, 128], P('dp', 'dap')
- pair_grad: bfloat16 [8, 128, 128, 128], P('dp', 'dap')
- proj_grad: float32 [128, 512], replicated
- gate_grad: float32 [128, 128], replicated
- out_grad: float32 [128, 128], replicated
- in_norm_grad: float32 [2, 128], replicated
- out_norm_grad: float32 [2, 128], replicated
All inputs are finite; a program needn't handle non-finite values.
Results may differ from a plain program's by a relative error of at most 0.0084.
Values may be sent and summed in bfloat16 or wider, within the bound.
A program may use at most 64 MiB of HBM per device.

v0:
```python
import jax
import jax.numpy as jnp
from jax import lax
from jax.sharding import PartitionSpec as P

epsilon = 1e-05


def norm_rows(values, along):
    row_mean = jnp.mean(values, axis=along, keepdims=True)
    centred = values - row_mean
    row_var = jnp.mean(centred * centred, axis=along, keepdims=True)
    inv_std = lax.rsqrt(row_var + epsilon)
    return (centred * inv_std, inv_std)


def norm_back(grad_hat, x_hat, inv_std, along):
    first = jnp.mean(grad_hat, axis=along, keepdims=True)
    second = jnp.mean(grad_hat * x_hat, axis=along, keepdims=True)
    return (grad_hat - first - x_hat * second) * inv_std


def backward_pieces(piece_d, piece_l, piece_r):
    back_l = jnp.einsum(
        "zhij,zhjk->zhik", piece_d, piece_r, preferred_element_type=jnp.float32
    ).astype(jnp.bfloat16)
    back_r = jnp.einsum(
        "zhij,zhik->zhjk", piece_d, piece_l, preferred_element_type=jnp.float32
    ).astype(jnp.bfloat16)
    return (back_l, back_r)


def shards(
    pair_act, pair_cot, in_gain, in_bias, proj_weight, gate_weight, out_gain, out_bias, out_weight
):
    f32 = jnp.float32
    bf16 = jnp.bfloat16
    groups = lax.axis_size("dap")
    row_count = pair_act.shape[1]
    crop_len = pair_act.shape[2]
    channels = pair_act.shape[3]
    hidden_w = out_weight.shape[0]
    per_dev = hidden_w // groups
    cell_count = row_count * crop_len
    scale = 1.0 / crop_len
    flat_act = pair_act.reshape(cell_count, channels).astype(f32)
    in_hat, in_inv = norm_rows(flat_act, 1)
    normed = (in_hat * in_gain + in_bias).astype(bf16)
    projected = jnp.einsum("mc,ch->hm", normed, proj_weight, preferred_element_type=f32)
    pre_ag = projected[0:hidden_w]
    pre_ap = projected[hidden_w : 2 * hidden_w]
    pre_bg = projected[2 * hidden_w : 3 * hidden_w]
    pre_bp = projected[3 * hidden_w : 4 * hidden_w]
    sig_a = jax.nn.sigmoid(pre_ag)
    sig_b = jax.nn.sigmoid(pre_bg)
    left_act = (sig_a * pre_ap).astype(bf16).reshape(groups, per_dev, row_count, crop_len)
    right_act = (sig_b * pre_bp).astype(bf16).reshape(groups, per_dev, row_count, crop_len)
    piece_l = lax.all_to_all(left_act, "dap", split_axis=0, concat_axis=2, tiled=True)
    piece_r = lax.all_to_all(right_act, "dap", split_axis=0, concat_axis=2, tiled=True)
    product = jnp.einsum("zhik,zhjk->zhij", piece_l, piece_r, preferred_element_type=f32).astype(
        bf16
    )
    returned = lax.all_to_all(product, "dap", split_axis=2, concat_axis=0, tiled=True)
    tri_out = returned.reshape(hidden_w, cell_count)
    tri_hat, tri_inv = norm_rows(tri_out.astype(f32), 0)
    tri_norm = (tri_hat * out_gain[:, None] + out_bias[:, None]).astype(bf16)
    gate_val = jax.nn.sigmoid(jnp.dot(normed, gate_weight, preferred_element_type=f32))
    mixed = jnp.einsum("hm,hc->mc", tri_norm, out_weight, preferred_element_type=f32)
    update = (gate_val * mixed).astype(bf16).reshape(1, row_count, crop_len, channels)
    cot_flat = pair_cot.reshape(cell_count, channels).astype(f32)
    d_mixed = (cot_flat * gate_val).astype(bf16)
    d_gate = (cot_flat * mixed * gate_val * (1.0 - gate_val)).astype(bf16)
    out_part = jnp.einsum("hm,mc->hc", tri_norm, d_mixed, preferred_element_type=f32) * scale
    gate_part = jnp.einsum("mc,md->cd", normed, d_gate, preferred_element_type=f32) * scale
    d_norm_out = jnp.einsum("mc,hc->hm", d_mixed, out_weight, preferred_element_type=f32)
    out_norm_part = (
        jnp.stack([jnp.sum(d_norm_out * tri_hat, axis=1), jnp.sum(d_norm_out, axis=1)]) * scale
    )
    d_tri = norm_back(d_norm_out * out_gain[:, None], tri_hat, tri_inv, 0).astype(bf16)
    d_tri = d_tri.reshape(groups, per_dev, row_count, crop_len)
    d_cols = lax.all_to_all(d_tri, "dap", split_axis=0, concat_axis=2, tiled=True)
    back_l, back_r = backward_pieces(d_cols, piece_l, piece_r)
    d_left, d_right = (
        lax.all_to_all(back_l, "dap", split_axis=2, concat_axis=0, tiled=True),
        lax.all_to_all(back_r, "dap", split_axis=2, concat_axis=0, tiled=True),
    )
    left_grad = d_left.reshape(hidden_w, cell_count).astype(f32)
    right_grad = d_right.reshape(hidden_w, cell_count).astype(f32)
    d_proj = jnp.concatenate(
        [
            left_grad * pre_ap * sig_a * (1.0 - sig_a),
            left_grad * sig_a,
            right_grad * pre_bp * sig_b * (1.0 - sig_b),
            right_grad * sig_b,
        ],
        axis=0,
    ).astype(bf16)
    proj_part = jnp.einsum("mc,hm->ch", normed, d_proj, preferred_element_type=f32) * scale
    d_normed = jnp.einsum(
        "hm,ch->mc", d_proj, proj_weight, preferred_element_type=f32
    ) + jnp.einsum("md,cd->mc", d_gate, gate_weight, preferred_element_type=f32)
    in_norm_part = (
        jnp.stack([jnp.sum(d_normed * in_hat, axis=0), jnp.sum(d_normed, axis=0)]) * scale
    )
    pair_grad = (
        norm_back(d_normed * in_gain, in_hat, in_inv, 1)
        .astype(bf16)
        .reshape(1, row_count, crop_len, channels)
    )
    proj_sum, gate_sum, out_sum, in_sum, outn_sum = lax.psum(
        (proj_part, gate_part, out_part, in_norm_part, out_norm_part), ("dp", "dap")
    )
    return (update, pair_grad, proj_sum, gate_sum, out_sum, in_sum, outn_sum)


def solution(mesh):
    placed = (
        P("dp", "dap", None, None),
        P("dp", "dap", None, None),
        P(),
        P(),
        P(),
        P(),
        P(),
        P(),
        P(),
    )
    return jax.shard_map(
        shards,
        mesh=mesh,
        in_specs=placed,
        out_specs=(P("dp", "dap", None, None), P("dp", "dap", None, None), P(), P(), P(), P(), P()),
        check_vma=False,
    )
```

profile of v0, /device:TPU:0, one launch (start us, length us, event | category | flops | bytes accessed | tf_op | source)
XLA Modules:
  0.0 383.8 jit_solution(13851624344998094155)
XLA Ops:
  7.2 1.7 convert_reduce_fusion
  8.9 2.3 multiply_reduce_fusion.3
  11.3 1.3 add_convert_fusion.1
  12.6 1.0 copy-done.5
  13.5 1.3 convolution_bitcast_fusion
  14.8 1.1 fusion.30
  15.9 2.1 copy-done.1
  18.1 1.2 copy.46
  19.3 6.3 %all-to-all-start.1 = ((bf16[4,32,32,128]{3,2,1,0:T(8,128)(2,1)}), bf16[4,32,32,128]{3,2,1,0:T(8,128)(2,1)S(1)}, u32[]{:S(2)}, u32[]{:S(2)}) async-start(bf16[4,32,32,128]{3,2,1,0:T(8,128)(2,1)} %bitcast.157), calls=%async_computation.1 | async-start | bytes 2097152 | tf_op jit(solution)/shard_map/all_to_all | solution.py:59
  25.6 1.2 copy.45
  26.8 24.5 %all-to-all-done.1 = bf16[4,32,32,128]{3,2,1,0:T(8,128)(2,1)S(1)} async-done(((bf16[4,32,32,128]{3,2,1,0:T(8,128)(2,1)}), bf16[4,32,32,128]{3,2,1,0:T(8,128)(2,1)S(1)}, u32[]{:S(2)}, u32[]{:S(2)}) %all-to-all-start.1) | async-done | bytes 1048608 | tf_op jit(solution)/shard_map/all_to_all | solution.py:59
  51.4 4.3 %all-to-all-start = ((bf16[4,32,32,128]{3,2,1,0:T(8,128)(2,1)}), bf16[4,32,32,128]{3,2,1,0:T(8,128)(2,1)}, u32[]{:S(2)}, u32[]{:S(2)}) async-start(bf16[4,32,32,128]{3,2,1,0:T(8,128)(2,1)} %bitcast.156), calls=%async_computation | async-start | bytes 2097152 | tf_op jit(solution)/shard_map/all_to_all | solution.py:58
  55.8 25.2 %all-to-all-done = bf16[4,32,32,128]{3,2,1,0:T(8,128)(2,1)} async-done(((bf16[4,32,32,128]{3,2,1,0:T(8,128)(2,1)}), bf16[4,32,32,128]{3,2,1,0:T(8,128)(2,1)}, u32[]{:S(2)}, u32[]{:S(2)}) %all-to-all-start) | async-done | bytes 1048608 | tf_op jit(solution)/shard_map/all_to_all | solution.py:58
  81.0 1.3 copy.32
  83.9 27.7 %all_to_all.72 = bf16[1,32,128,128]{3,1,0,2:T(8,128)(2,1)S(1)} all-to-all(bf16[1,32,128,128]{3,1,0,2:T(8,128)(2,1)S(1)} %copy.34), channel_id=1, replica_groups=mesh['dp'=8,'dap'=4] {'dap'}, dimensions={2} | all-to-all | bytes 2097152 | tf_op jit(solution)/shard_map/all_to_all | solution.py:63
  112.2 1.1 bitcast_reduce_fusion
  113.4 1.1 fusion.23
  114.5 3.0 copy.58
  117.5 1.9 copy.36
  119.4 2.3 add_convert_fusion
  121.8 1.0 copy-done.12
  124.3 2.7 fusion.6
  127.0 2.4 fusion.21
  129.4 1.3 copy-done.3
  130.8 4.1 %multiply_convert_fusion.1 = bf16[128,4096]{0,1:T(8,128)(2,1)} fusion(f32[4096,128]{1,0:T(8,128)S(1)} %get-tuple-element.34, f32[128,4096]{0,1:T(8,128)S(1)} %copy.36, f32[4096]{0:T(1024)S(1)} %get-tuple-element.36, f32[4096]{0:T(1024)S(1)} %get-tuple-element.37, f32[128]{0:T(128)S(1)} %copy-done.22, f32[4096]{0:T(1024)S(1)} %rsqrt_bitcast_fusion, ...), kind=kLoop, calls=%fused_computation.46 | loop fusion | flops 4194304 | bytes 5308928 | tf_op jit(solution)/shard_map/convert_element_type | solution.py:79
  134.8 1.5 copy.37
  136.6 27.8 %all_to_all.73 = bf16[4,32,32,128]{3,2,1,0:T(8,128)(2,1)S(1)} all-to-all(bf16[4,32,32,128]{3,2,1,0:T(8,128)(2,1)S(1)} %bitcast.159), channel_id=1, replica_groups=mesh['dp'=8,'dap'=4] {'dap'}, dimensions={0} | all-to-all | bytes 2097152 | tf_op jit(solution)/shard_map/all_to_all | solution.py:81
  165.0 1.7 copy.39
  166.6 4.3 %all-to-all-start.4 = ((bf16[1,32,128,128]{3,1,0,2:T(8,128)(2,1)}), bf16[1,32,128,128]{3,1,0,2:T(8,128)(2,1)}, u32[]{:S(2)}, u32[]{:S(2)}) async-start(bf16[1,32,128,128]{3,1,0,2:T(8,128)(2,1)} %copy.39), calls=%async_computation.4 | async-start | bytes 2097152 | tf_op jit(solution)/shard_map/all_to_all | solution.py:84
  171.4 1.7 copy.42
  173.1 22.6 %all-to-all-done.4 = bf16[1,32,128,128]{3,1,0,2:T(8,128)(2,1)} async-done(((bf16[1,32,128,128]{3,1,0,2:T(8,128)(2,1)}), bf16[1,32,128,128]{3,1,0,2:T(8,128)(2,1)}, u32[]{:S(2)}, u32[]{:S(2)}) %all-to-all-start.4) | async-done | bytes 1048608 | tf_op jit(solution)/shard_map/all_to_all | solution.py:84
  195.7 4.5 %all-to-all-start.5 = ((bf16[1,32,128,128]{3,1,0,2:T(8,128)(2,1)}), bf16[1,32,128,128]{3,1,0,2:T(8,128)(2,1)}, u32[]{:S(2)}, u32[]{:S(2)}) async-start(bf16[1,32,128,128]{3,1,0,2:T(8,128)(2,1)} %copy.42), calls=%async_computation.5 | async-start | bytes 2097152 | tf_op jit(solution)/shard_map/all_to_all | solution.py:85
  200.8 2.8 convolution_multiply_fusion.1
  203.6 1.1 convolution_multiply_fusion.2
  204.7 2.9 copy.40
  207.7 17.9 %all-to-all-done.5 = bf16[1,32,128,128]{3,1,0,2:T(8,128)(2,1)} async-done(((bf16[1,32,128,128]{3,1,0,2:T(8,128)(2,1)}), bf16[1,32,128,128]{3,1,0,2:T(8,128)(2,1)}, u32[]{:S(2)}, u32[]{:S(2)}) %all-to-all-start.5) | async-done | bytes 1048608 | tf_op jit(solution)/shard_map/all_to_all | solution.py:85
  225.5 1.7 copy.43
  227.4 6.3 %fusion.13 = (bf16[128,4096]{1,0:T(8,128)(2,1)S(1)}, bf16[128,4096]{1,0:T(8,128)(2,1)S(1)}, bf16[128,4096]{1,0:T(8,128)(2,1)S(1)}, bf16[128,4096]{1,0:T(8,128)(2,1)S(1)}) fusion(f32[16,8,32,128]{3,2,1,0:T(8,128)S(1)} %bitcast.153, f32[512,4096]{1,0:T(8,128)} %copy-done.1, f32[16,8,32,128]{3,2,1,0:T(8,128)S(1)} %bitcast.154), kind=kLoop, calls=%fused_computation.23 | loop fusion | flops 10485760 | bytes 16777216 | tf_op jit(solution)/shard_map/convert.13
  233.8 1.0 copy-done.17
  235.4 2.2 convolution_multiply_fusion
  237.6 3.0 fusion.31
  240.6 2.4 multiply_reduce_fusion
  243.1 3.3 multiply_convert_fusion
  246.3 37.9 %all-reduce = (f32[2,128]{1,0:T(2,128)}, f32[2,128]{1,0:T(2,128)}) all-reduce(f32[2,128]{1,0:T(2,128)S(1)} %maximum_multiply_fusion, f32[2,128]{1,0:T(2,128)S(1)} %maximum_multiply_fusion.1), channel_id=1, replica_groups=mesh['dp'=8,'dap'=4] {'dp','dap'}, use_global_device_ids=true, to_apply=%region_13.0 | all-reduce | flops 512 | bytes 4096 | tf_op jit(solution)/shard_map/psum | solution.py:110
  284.3 88.0 %all-reduce.4.cloned.1.call-done = (f32[128,512]{1,0:T(8,128)}, f32[128,128]{1,0:T(8,128)}, f32[128,128]{1,0:T(8,128)}) async-done(((f32[128,512]{1,0:T(8,128)}, f32[128,128]{1,0:T(8,128)}, f32[128,128]{1,0:T(8,128)}), (f32[128,512]{1,0:T(8,128)}, f32[128,128]{1,0:T(8,128)}, f32[128,128]{1,0:T(8,128)})) %all-reduce.4.cloned.1.call-update) | async-done | bytes 393232 | tf_op jit(solution)/shard_map/psum | solution.py:110
  372.3 1.7 copy.62
  374.0 1.5 copy.63
  375.5 1.5 copy.64
  (71 shorter events, 6.8 us)
Async XLA Ops:
  7.2 6.4 %copy-start = (bf16[128,512]{1,0:T(8,128)(2,1)S(1)}, bf16[128,512]{1,0:T(8,128)(2,1)}, u32[]{:S(2)}) copy-start(bf16[128,512]{1,0:T(8,128)(2,1)} %param.13) | copy-start | bytes 393220
  7.2 4.1 %copy-start.2 = (bf16[1,32,128,128]{3,2,1,0:T(8,128)(2,1)S(1)}, bf16[1,32,128,128]{3,2,1,0:T(8,128)(2,1)}, u32[]{:S(2)}) copy-start(bf16[1,32,128,128]{3,2,1,0:T(8,128)(2,1)} %param.9) | copy-start | bytes 3145732
  7.2 4.1 %copy-start.23 = (f32[128]{0:T(128)S(1)}, f32[128]{0:T(128)}, u32[]{:S(2)}) copy-start(f32[128]{0:T(128)} %param.11) | copy-start | bytes 1540
  7.2 4.1 %copy-start.25 = (f32[128]{0:T(128)S(1)}, f32[128]{0:T(128)}, u32[]{:S(2)}) copy-start(f32[128]{0:T(128)} %param.12) | copy-start | bytes 1540
  12.6 1.0 copy-start.5
  14.8 3.2 copy-start.1
  19.3 32.1 %all-to-all-start.1 = ((bf16[4,32,32,128]{3,2,1,0:T(8,128)(2,1)}), bf16[4,32,32,128]{3,2,1,0:T(8,128)(2,1)S(1)}, u32[]{:S(2)}, u32[]{:S(2)}) async-start(bf16[4,32,32,128]{3,2,1,0:T(8,128)(2,1)} %bitcast.157), calls=%async_computation.1 | async-start | bytes 2097152 | tf_op jit(solution)/shard_map/all_to_all | solution.py:59
  51.4 29.6 %all-to-all-start = ((bf16[4,32,32,128]{3,2,1,0:T(8,128)(2,1)}), bf16[4,32,32,128]{3,2,1,0:T(8,128)(2,1)}, u32[]{:S(2)}, u32[]{:S(2)}) async-start(bf16[4,32,32,128]{3,2,1,0:T(8,128)(2,1)} %bitcast.156), calls=%async_computation | async-start | bytes 2097152 | tf_op jit(solution)/shard_map/all_to_all | solution.py:58
  55.8 27.4 %copy-start.10 = (bf16[1,32,4,32,128]{4,3,2,1,0:T(8,128)(2,1)}, bf16[1,32,4,32,128]{4,3,2,1,0:T(8,128)(2,1)S(1)}, u32[]{:S(2)}) copy-start(bf16[1,32,4,32,128]{4,3,2,1,0:T(8,128)(2,1)S(1)} %copy.33) | copy-start | bytes 3145732
  82.3 1.6 copy-start.8
  117.5 2.0 copy-start.22
  117.5 2.0 copy-start.24
  119.4 3.3 copy-start.20
  121.7 1.0 copy-start.12
  122.7 1.2 copy-start.6
  122.7 1.2 copy-start.21
  122.8 1.6 copy-start.26
  127.0 2.4 copy-start.16
  129.4 1.4 copy-start.3
  136.6 27.9 %copy-start.11 = (bf16[1,32,4,32,128]{4,3,2,1,0:T(8,128)(2,1)S(1)}, bf16[1,32,4,32,128]{4,3,2,1,0:T(8,128)(2,1)}, u32[]{:S(2)}) copy-start(bf16[1,32,4,32,128]{4,3,2,1,0:T(8,128)(2,1)} %copy-done.10) | copy-start | bytes 3145732
  165.0 5.9 %copy-start.9 = (bf16[1,32,4,32,128]{4,3,2,1,0:T(8,128)(2,1)S(1)}, bf16[1,32,4,32,128]{4,3,2,1,0:T(8,128)(2,1)}, u32[]{:S(2)}) copy-start(bf16[1,32,4,32,128]{4,3,2,1,0:T(8,128)(2,1)} %copy-done.8) | copy-start | bytes 3145732
  166.6 29.1 %all-to-all-start.4 = ((bf16[1,32,128,128]{3,1,0,2:T(8,128)(2,1)}), bf16[1,32,128,128]{3,1,0,2:T(8,128)(2,1)}, u32[]{:S(2)}, u32[]{:S(2)}) async-start(bf16[1,32,128,128]{3,1,0,2:T(8,128)(2,1)} %copy.39), calls=%async_computation.4 | async-start | bytes 2097152 | tf_op jit(solution)/shard_map/all_to_all | solution.py:84
  171.4 28.8 %copy-start.4 = (f32[4096,128]{1,0:T(8,128)S(1)}, f32[4096,128]{1,0:T(8,128)}, u32[]{:S(2)}) copy-start(f32[4096,128]{1,0:T(8,128)} %copy-done.3) | copy-start | bytes 6291460
  195.7 29.8 %all-to-all-start.5 = ((bf16[1,32,128,128]{3,1,0,2:T(8,128)(2,1)}), bf16[1,32,128,128]{3,1,0,2:T(8,128)(2,1)}, u32[]{:S(2)}, u32[]{:S(2)}) async-start(bf16[1,32,128,128]{3,1,0,2:T(8,128)(2,1)} %copy.42), calls=%async_computation.5 | async-start | bytes 2097152 | tf_op jit(solution)/shard_map/all_to_all | solution.py:85
  200.2 172.1 %all-reduce.4.cloned.1.call-start = ((), (), s32[]{:S(2)}) async-start(), calls=%async_computation.6 | async-start | bytes 786432 | tf_op jit(solution)/shard_map/psum | solution.py:110
  200.8 2.8 copy-start.7
  200.8 2.8 copy-start.14
  225.5 1.9 copy-start.13
  233.7 1.0 copy-start.17
  233.8 1.3 copy-start.18
  233.8 1.6 copy-start.19
  237.6 3.0 copy-start.15
Sparse Core Ops, SparseCore 0:
  243.2 129.0 all-reduce.3
where the time goes:
time: 385 us; the launch traced here: 384 us
  waiting for transfers between devices  178 us (46%)
  blocking collectives  93.5 us (24%)
  local copies, waits for them, and re-layouts  32.7 us (8%)
  other arithmetic  25.3 us (7%)
  matrix products  20.1 us (5%)
  starting transfers between devices  19.4 us (5%)
  between operations  14.6 us (4%)
    psum x1, waiting for transfers between devices, shards(): lax.psum((proj_part, gate_part, out_part, in_norm_part, out_norm_part), (...  88 us
    psum x1, blocking collectives, shards(): lax.psum((proj_part, gate_part, out_part, in_norm_part, out_norm_part), (...  37.9 us
    all_to_all x1, blocking collectives, shards(): lax.all_to_all(d_tri, 'dap', split_axis=0, concat_axis=2, tiled=True)  27.8 us
    all_to_all x1, blocking collectives, shards(): lax.all_to_all(product, 'dap', split_axis=2, concat_axis=0, tiled=True)  27.7 us
    all_to_all x1, waiting for transfers between devices, shards(): lax.all_to_all(left_act, 'dap', split_axis=0, concat_axis=2, tiled=True)  25.2 us
    all_to_all x1, waiting for transfers between devices, shards(): lax.all_to_all(right_act, 'dap', split_axis=0, concat_axis=2, tiled=True)  24.5 us
    all_to_all x1, waiting for transfers between devices, shards(): lax.all_to_all(back_l, 'dap', split_axis=2, concat_axis=0, tiled=True)  22.6 us
    unnamed x61, local copies, waits for them, and re-layouts  18.7 us
  transfers between devices with their start and end apart: 5, of which 5 were waited for; matrix products, arithmetic and copies ran while one was open for 4% of the time, Pallas kernels for 0%

commit v1 on v0

--- a/solution.py
+++ b/solution.py
@@ -4,6 +4,18 @@
 from jax.sharding import PartitionSpec as P
 
 epsilon = 1e-05
+
+
+def cut_along(array, dim, size):
+    shape = array.shape
+    blocks = array.reshape(*shape[:dim], size, shape[dim] // size, *shape[dim + 1 :])
+    return jnp.moveaxis(blocks, dim, 0)
+
+
+def in_order(parts, dim):
+    parts = jnp.moveaxis(parts, 0, dim)
+    shape = parts.shape
+    return parts.reshape(*shape[:dim], shape[dim] * shape[dim + 1], *shape[dim + 2 :])
 
 
 def norm_rows(values, along):
@@ -60,7 +72,15 @@
     product = jnp.einsum("zhik,zhjk->zhij", piece_l, piece_r, preferred_element_type=f32).astype(
         bf16
     )
-    returned = lax.all_to_all(product, "dap", split_axis=2, concat_axis=0, tiled=True)
+    devices, index = (lax.axis_size("dap"), lax.axis_index("dap"))
+    blocks = cut_along(product, 2, devices)
+    filled = blocks
+    for step in range(1, devices):
+        target, source = ((index + step) % devices, (index - step) % devices)
+        sent = lax.dynamic_index_in_dim(blocks, target, 0)
+        other = lax.ppermute(sent, "dap", [(i, (i + step) % devices) for i in range(devices)])
+        filled = lax.dynamic_update_slice_in_dim(filled, other, source, axis=0)
+    returned = in_order(filled, 0)
     tri_out = returned.reshape(hidden_w, cell_count)
     tri_hat, tri_inv = norm_rows(tri_out.astype(f32), 0)
     tri_norm = (tri_hat * out_gain[:, None] + out_bias[:, None]).astype(bf16)

time: 385 us -> 379 us (0.984)
  blocking collectives: 93.5 us -> 69.5 us
  waiting for transfers between devices: 178 us -> 192 us
    all_to_all x1 -> x0, blocking collectives: 27.7 us -> none  [shards(): lax.all_to_all(product, 'dap', split_axis=2, concat_axis=0, tiled=True)]
    ppermute x0 -> x3, waiting for transfers between devices: none -> 17.2 us  [shards(): lax.ppermute(sent, 'dap', [(i, (i + step) % devices) for i in range(devic...]
  transfers between devices with their start and end apart: 5 -> 8, of which waited for: 5 -> 7; matrix products, arithmetic and copies ran while one was open for 4% -> 6% of each run, Pallas kernels for 0% -> 0%
where the time goes in v1:
time: 379 us; the launch traced here: 378 us
  waiting for transfers between devices  192 us (51%)
  blocking collectives  69.5 us (18%)
  local copies, waits for them, and re-layouts  34 us (9%)
  other arithmetic  25 us (7%)
  matrix products  22.4 us (6%)
  starting transfers between devices  20.4 us (5%)
  between operations  14.6 us (4%)
    psum x1, waiting for transfers between devices, shards(): lax.psum((proj_part, gate_part, out_part, in_norm_part, out_norm_part), (...  86.6 us
    psum x1, blocking collectives, shards(): lax.psum((proj_part, gate_part, out_part, in_norm_part, out_norm_part), (...  37.9 us
    all_to_all x1, blocking collectives, shards(): lax.all_to_all(d_tri, 'dap', split_axis=0, concat_axis=2, tiled=True)  31.6 us
    all_to_all x1, waiting for transfers between devices, shards(): lax.all_to_all(right_act, 'dap', split_axis=0, concat_axis=2, tiled=True)  24.6 us
    all_to_all x1, waiting for transfers between devices, shards(): lax.all_to_all(back_l, 'dap', split_axis=2, concat_axis=0, tiled=True)  23.1 us
    all_to_all x1, waiting for transfers between devices, shards(): lax.all_to_all(left_act, 'dap', split_axis=0, concat_axis=2, tiled=True)  22.9 us
    all_to_all x1, waiting for transfers between devices, shards(): lax.all_to_all(back_r, 'dap', split_axis=2, concat_axis=0, tiled=True)  17.9 us
    ppermute x3, waiting for transfers between devices, shards(): lax.ppermute(sent, 'dap', [(i, (i + step) % devices) for i in range(devic...  17.2 us
  transfers between devices with their start and end apart: 8, of which 7 were waited for; matrix products, arithmetic and copies ran while one was open for 6% of the time, Pallas kernels for 0%

profile of v1, /device:TPU:0, one launch (start us, length us, event | category | flops | bytes accessed | tf_op | source)
XLA Modules:
  0.0 378.3 jit_solution(1075280760109512975)
XLA Ops:
  7.2 1.7 convert_reduce_fusion
  8.9 2.3 multiply_reduce_fusion.4
  11.3 1.3 add_convert_fusion.1
  12.6 1.3 convolution_bitcast_fusion
  13.9 1.1 fusion.27
  15.0 2.1 copy-done.1
  17.1 1.2 copy.45
  18.3 6.3 %all-to-all-start.1 = ((bf16[4,32,32,128]{3,2,1,0:T(8,128)(2,1)}), bf16[4,32,32,128]{3,2,1,0:T(8,128)(2,1)}, u32[]{:S(2)}, u32[]{:S(2)}) async-start(bf16[4,32,32,128]{3,2,1,0:T(8,128)(2,1)} %bitcast.158), calls=%async_computation.1 | async-start | bytes 2097152 | tf_op jit(solution)/shard_map/all_to_all | solution.py:71
  24.6 1.2 copy.44
  25.8 24.6 %all-to-all-done.1 = bf16[4,32,32,128]{3,2,1,0:T(8,128)(2,1)} async-done(((bf16[4,32,32,128]{3,2,1,0:T(8,128)(2,1)}), bf16[4,32,32,128]{3,2,1,0:T(8,128)(2,1)}, u32[]{:S(2)}, u32[]{:S(2)}) %all-to-all-start.1) | async-done | bytes 1048608 | tf_op jit(solution)/shard_map/all_to_all | solution.py:71
  50.5 3.5 all-to-all-start
  54.0 2.3 copy.33
  56.4 22.9 %all-to-all-done = bf16[4,32,32,128]{3,2,1,0:T(8,128)(2,1)S(1)} async-done(((bf16[4,32,32,128]{3,2,1,0:T(8,128)(2,1)}), bf16[4,32,32,128]{3,2,1,0:T(8,128)(2,1)S(1)}, u32[]{:S(2)}, u32[]{:S(2)}) %all-to-all-start) | async-done | bytes 1048608 | tf_op jit(solution)/shard_map/all_to_all | solution.py:70
  79.4 1.5 copy-done.9
  82.6 1.5 collective-permute-start.2
  84.6 2.1 fusion.2
  86.8 13.9 %collective-permute-done = bf16[1,1,32,32,128]{4,3,2,0,1:T(8,128)(2,1)} collective-permute-done((bf16[1,1,32,32,128]{4,3,2,0,1:T(8,128)(2,1)}, bf16[1,1,32,32,128]{4,3,2,0,1:T(8,128)(2,1)}, u32[]{:S(2)}, u32[]{:S(2)}) %collective-permute-start) | collective-permute-done | bytes 262176 | tf_op jit(solution)/shard_map/ppermute | solution.py:81
  101.7 3.4 collective-permute-done.1
  106.0 1.0 constant_dynamic-update-slice_fusion
  107.5 1.7 copy.56
  109.3 1.9 copy.35
  111.3 2.3 add_convert_fusion
  113.6 2.2 fusion.6
  115.8 2.5 fusion.21
  118.3 1.3 copy-done.3
  119.7 4.1 %multiply_convert_fusion.1 = bf16[128,4096]{0,1:T(8,128)(2,1)} fusion(f32[4096,128]{1,0:T(8,128)S(1)} %get-tuple-element.37, f32[128,4096]{0,1:T(8,128)S(1)} %copy.35, f32[4096]{0:T(1024)S(1)} %get-tuple-element.39, f32[4096]{0:T(1024)S(1)} %get-tuple-element.40, f32[128]{0:T(128)S(1)} %copy-done.23, f32[4096]{0:T(1024)S(1)} %rsqrt_bitcast_fusion, ...), kind=kLoop, calls=%fused_computation.42 | loop fusion | flops 4194304 | bytes 5308928 | tf_op jit(solution)/shard_map/convert_element_type | solution.py:99
  123.8 1.5 copy.36
  125.5 31.6 %all_to_all.63 = bf16[4,32,32,128]{3,2,1,0:T(8,128)(2,1)S(1)} all-to-all(bf16[4,32,32,128]{3,2,1,0:T(8,128)(2,1)S(1)} %bitcast.160), channel_id=1, replica_groups=mesh['dp'=8,'dap'=4] {'dap'}, dimensions={0} | all-to-all | bytes 2097152 | tf_op jit(solution)/shard_map/all_to_all | solution.py:101
  157.7 1.6 copy.38
  159.4 4.3 %all-to-all-start.3 = ((bf16[1,32,128,128]{3,1,0,2:T(8,128)(2,1)}), bf16[1,32,128,128]{3,1,0,2:T(8,128)(2,1)}, u32[]{:S(2)}, u32[]{:S(2)}) async-start(bf16[1,32,128,128]{3,1,0,2:T(8,128)(2,1)} %copy.38), calls=%async_computation.3 | async-start | bytes 2097152 | tf_op jit(solution)/shard_map/all_to_all | solution.py:104
  164.2 1.7 copy.41
  165.8 23.1 %all-to-all-done.3 = bf16[1,32,128,128]{3,1,0,2:T(8,128)(2,1)} async-done(((bf16[1,32,128,128]{3,1,0,2:T(8,128)(2,1)}), bf16[1,32,128,128]{3,1,0,2:T(8,128)(2,1)}, u32[]{:S(2)}, u32[]{:S(2)}) %all-to-all-start.3) | async-done | bytes 1048608 | tf_op jit(solution)/shard_map/all_to_all | solution.py:104
  189.0 4.3 %all-to-all-start.4 = ((bf16[1,32,128,128]{3,1,0,2:T(8,128)(2,1)}), bf16[1,32,128,128]{3,1,0,2:T(8,128)(2,1)}, u32[]{:S(2)}, u32[]{:S(2)}) async-start(bf16[1,32,128,128]{3,1,0,2:T(8,128)(2,1)} %copy.41), calls=%async_computation.4 | async-start | bytes 2097152 | tf_op jit(solution)/shard_map/all_to_all | solution.py:105
  193.9 2.8 convolution_multiply_fusion.1
  196.7 1.1 convolution_multiply_fusion.2
  197.8 2.9 copy.39
  200.7 17.9 %all-to-all-done.4 = bf16[1,32,128,128]{3,1,0,2:T(8,128)(2,1)} async-done(((bf16[1,32,128,128]{3,1,0,2:T(8,128)(2,1)}), bf16[1,32,128,128]{3,1,0,2:T(8,128)(2,1)}, u32[]{:S(2)}, u32[]{:S(2)}) %all-to-all-start.4) | async-done | bytes 1048608 | tf_op jit(solution)/shard_map/all_to_all | solution.py:105
  218.6 1.7 copy.42
  220.5 6.3 %fusion.13 = (bf16[128,4096]{1,0:T(8,128)(2,1)S(1)}, bf16[128,4096]{1,0:T(8,128)(2,1)S(1)}, bf16[128,4096]{1,0:T(8,128)(2,1)S(1)}, bf16[128,4096]{1,0:T(8,128)(2,1)S(1)}) fusion(f32[16,8,32,128]{3,2,1,0:T(8,128)S(1)} %bitcast.152, f32[512,4096]{1,0:T(8,128)} %copy-done.1, f32[16,8,32,128]{3,2,1,0:T(8,128)S(1)} %bitcast.153), kind=kLoop, calls=%fused_computation.23 | loop fusion | flops 10485760 | bytes 16777216 | tf_op jit(solution)/shard_map/convert.9
  228.8 2.2 convolution_multiply_fusion
  231.0 3.0 fusion.28
  234.1 3.4 multiply_reduce_fusion
  237.5 4.8 %multiply_convert_fusion = bf16[4096,128]{1,0:T(8,128)(2,1)} fusion(f32[4096,128]{1,0:T(8,128)} %get-tuple-element.38, bf16[1,32,128,128]{3,2,1,0:T(8,128)(2,1)S(1)} %copy-done.2, f32[4096]{0:T(1024)S(1)} %broadcast_multiply_fusion, f32[4096]{0:T(1024)S(1)} %broadcast_multiply_fusion.1, f32[128]{0:T(128)S(1)} %copy-done.24, ...), kind=kLoop, calls=%fused_computation.40 | loop fusion | flops 4718592 | bytes 4260352 | tf_op jit(solution)/shard_map/convert_element_type | solution.py:127
  242.3 37.9 %all-reduce = (f32[2,128]{1,0:T(2,128)}, f32[2,128]{1,0:T(2,128)}) all-reduce(f32[2,128]{1,0:T(2,128)S(1)} %maximum_multiply_fusion, f32[2,128]{1,0:T(2,128)S(1)} %maximum_multiply_fusion.1), channel_id=1, replica_groups=mesh['dp'=8,'dap'=4] {'dp','dap'}, use_global_device_ids=true, to_apply=%region_13.14 | all-reduce | flops 512 | bytes 4096 | tf_op jit(solution)/shard_map/psum | solution.py:130
  280.2 86.6 %all-reduce.4.cloned.1.call-done = (f32[128,512]{1,0:T(8,128)}, f32[128,128]{1,0:T(8,128)}, f32[128,128]{1,0:T(8,128)}) async-done(((f32[128,512]{1,0:T(8,128)}, f32[128,128]{1,0:T(8,128)}, f32[128,128]{1,0:T(8,128)}), (f32[128,512]{1,0:T(8,128)}, f32[128,128]{1,0:T(8,128)}, f32[128,128]{1,0:T(8,128)})) %all-reduce.4.cloned.1.call-update) | async-done | bytes 393232 | tf_op jit(solution)/shard_map/psum | solution.py:130
  366.8 1.7 copy.64
  368.5 1.5 copy.65
  369.9 1.5 copy.66
  (78 shorter events, 9.2 us)
Async XLA Ops:
  7.2 5.4 %copy-start = (bf16[128,512]{1,0:T(8,128)(2,1)S(1)}, bf16[128,512]{1,0:T(8,128)(2,1)}, u32[]{:S(2)}) copy-start(bf16[128,512]{1,0:T(8,128)(2,1)} %param.13) | copy-start | bytes 393220
  7.2 4.1 %copy-start.2 = (bf16[1,32,128,128]{3,2,1,0:T(8,128)(2,1)S(1)}, bf16[1,32,128,128]{3,2,1,0:T(8,128)(2,1)}, u32[]{:S(2)}) copy-start(bf16[1,32,128,128]{3,2,1,0:T(8,128)(2,1)} %param.9) | copy-start | bytes 3145732
  7.2 4.1 %copy-start.24 = (f32[128]{0:T(128)S(1)}, f32[128]{0:T(128)}, u32[]{:S(2)}) copy-start(f32[128]{0:T(128)} %param.11) | copy-start | bytes 1540
  7.2 4.1 %copy-start.26 = (f32[128]{0:T(128)S(1)}, f32[128]{0:T(128)}, u32[]{:S(2)}) copy-start(f32[128]{0:T(128)} %param.12) | copy-start | bytes 1540
  12.6 72.1 %copy-start.5 = (bf16[4096,128]{1,0:T(8,128)(2,1)}, bf16[4096,128]{1,0:T(8,128)(2,1)S(1)}, u32[]{:S(2)}) copy-start(bf16[4096,128]{1,0:T(8,128)(2,1)S(1)} %add_convert_fusion.1) | copy-start | bytes 3145732
  13.9 3.2 copy-start.1
  18.3 32.2 %all-to-all-start.1 = ((bf16[4,32,32,128]{3,2,1,0:T(8,128)(2,1)}), bf16[4,32,32,128]{3,2,1,0:T(8,128)(2,1)}, u32[]{:S(2)}, u32[]{:S(2)}) async-start(bf16[4,32,32,128]{3,2,1,0:T(8,128)(2,1)} %bitcast.158), calls=%async_computation.1 | async-start | bytes 2097152 | tf_op jit(solution)/shard_map/all_to_all | solution.py:71
  50.5 28.8 %all-to-all-start = ((bf16[4,32,32,128]{3,2,1,0:T(8,128)(2,1)}), bf16[4,32,32,128]{3,2,1,0:T(8,128)(2,1)S(1)}, u32[]{:S(2)}, u32[]{:S(2)}) async-start(bf16[4,32,32,128]{3,2,1,0:T(8,128)(2,1)} %bitcast.156), calls=%async_computation | async-start | bytes 2097152 | tf_op jit(solution)/shard_map/all_to_all | solution.py:70
  79.2 1.6 copy-start.9
  79.4 3.2 copy-start.7
  80.9 3.8 %copy-start.22 = (bf16[128,128]{1,0:T(8,128)(2,1)S(1)}, bf16[128,128]{1,0:T(8,128)(2,1)}, u32[]{:S(2)}) copy-start(bf16[128,128]{1,0:T(8,128)(2,1)} %param.14) | copy-start | bytes 98308
  82.6 23.4 %collective-permute-start.2 = (bf16[1,1,32,32,128]{4,3,2,0,1:T(8,128)(2,1)}, bf16[1,1,32,32,128]{4,3,2,0,1:T(8,128)(2,1)}, u32[]{:S(2)}, u32[]{:S(2)}) collective-permute-start(bf16[1,1,32,32,128]{4,3,2,0,1:T(8,128)(2,1)} %get-tuple-element.30), channel_id=1, source_target_pairs={{0,3},{1,0},{2,1},{3,2},{4,7},{5,4},{6,5},{7,6},{8,11},{9,8},{10,9... | collective-permute-start | bytes 786440 | tf_op jit(solution)/shard_map/ppermute | solution.py:81
  84.1 20.9 %collective-permute-start.1 = (bf16[1,1,32,32,128]{4,3,2,0,1:T(8,128)(2,1)}, bf16[1,1,32,32,128]{4,3,2,0,1:T(8,128)(2,1)}, u32[]{:S(2)}, u32[]{:S(2)}) collective-permute-start(bf16[1,1,32,32,128]{4,3,2,0,1:T(8,128)(2,1)} %get-tuple-element.31), channel_id=1, source_target_pairs={{0,2},{1,3},{2,0},{3,1},{4,6},{5,7},{6,4},{7,5},{8,10},{9,11},{10,... | collective-permute-start | bytes 786440 | tf_op jit(solution)/shard_map/ppermute | solution.py:81
  84.1 16.6 %collective-permute-start = (bf16[1,1,32,32,128]{4,3,2,0,1:T(8,128)(2,1)}, bf16[1,1,32,32,128]{4,3,2,0,1:T(8,128)(2,1)}, u32[]{:S(2)}, u32[]{:S(2)}) collective-permute-start(bf16[1,1,32,32,128]{4,3,2,0,1:T(8,128)(2,1)} %get-tuple-element.32), channel_id=1, source_target_pairs={{0,1},{1,2},{2,3},{3,0},{4,5},{5,6},{6,7},{7,4},{8,9},{9,10},{10,1... | collective-permute-start | bytes 786440 | tf_op jit(solution)/shard_map/ppermute | solution.py:81
  109.3 2.0 copy-start.23
  109.3 2.0 copy-start.25
  111.2 2.4 copy-start.15
  111.2 2.4 copy-start.16
  111.2 2.4 copy-start.21
  113.6 2.2 copy-start.11
  115.8 2.5 copy-start.13
  118.3 1.4 copy-start.3
  125.5 31.8 %copy-start.10 = (bf16[1,32,4,32,128]{4,3,2,1,0:T(8,128)(2,1)S(1)}, bf16[1,32,4,32,128]{4,3,2,1,0:T(8,128)(2,1)}, u32[]{:S(2)}) copy-start(bf16[1,32,4,32,128]{4,3,2,1,0:T(8,128)(2,1)} %copy.33) | copy-start | bytes 3145732
  157.7 5.9 %copy-start.8 = (bf16[1,32,4,32,128]{4,3,2,1,0:T(8,128)(2,1)S(1)}, bf16[1,32,4,32,128]{4,3,2,1,0:T(8,128)(2,1)}, u32[]{:S(2)}) copy-start(bf16[1,32,4,32,128]{4,3,2,1,0:T(8,128)(2,1)} %copy-done.7) | copy-start | bytes 3145732
  159.4 29.6 %all-to-all-start.3 = ((bf16[1,32,128,128]{3,1,0,2:T(8,128)(2,1)}), bf16[1,32,128,128]{3,1,0,2:T(8,128)(2,1)}, u32[]{:S(2)}, u32[]{:S(2)}) async-start(bf16[1,32,128,128]{3,1,0,2:T(8,128)(2,1)} %copy.38), calls=%async_computation.3 | async-start | bytes 2097152 | tf_op jit(solution)/shard_map/all_to_all | solution.py:104
  164.2 29.1 %copy-start.4 = (f32[4096,128]{1,0:T(8,128)S(1)}, f32[4096,128]{1,0:T(8,128)}, u32[]{:S(2)}) copy-start(f32[4096,128]{1,0:T(8,128)} %copy-done.3) | copy-start | bytes 6291460
  189.0 29.6 %all-to-all-start.4 = ((bf16[1,32,128,128]{3,1,0,2:T(8,128)(2,1)}), bf16[1,32,128,128]{3,1,0,2:T(8,128)(2,1)}, u32[]{:S(2)}, u32[]{:S(2)}) async-start(bf16[1,32,128,128]{3,1,0,2:T(8,128)(2,1)} %copy.41), calls=%async_computation.4 | async-start | bytes 2097152 | tf_op jit(solution)/shard_map/all_to_all | solution.py:105
  193.2 173.5 %all-reduce.4.cloned.1.call-start = ((), (), s32[]{:S(2)}) async-start(), calls=%async_computation.5 | async-start | bytes 786432 | tf_op jit(solution)/shard_map/psum | solution.py:130
  193.9 2.8 copy-start.6
  193.9 2.8 copy-start.12
  218.6 1.9 copy-start.14
  226.8 1.0 copy-start.17
  226.8 1.3 copy-start.18
  226.8 1.6 copy-start.19
  226.8 2.0 copy-start.20
Sparse Core Ops, SparseCore 0:
  237.7 129.0 all-reduce.3
